TPU v7x, 32 devices: a whole 2x2x4 slice. The times are simulated.
32 devices in a mesh: dp: 8 (over z, x), segment: 2 (over y), mp: 2 (over core).
Axes of the slice: x: 2, y: 2, z: 4, core: 2. Of those that a mesh axis runs over, the one named last changes fastest.
Arguments:
- prefix_hidden: bfloat16 [16, 512, 8192], P(('dp', 'segment'), 'mp'), may hold values from -6 to 6
- norm_gain: float32 [8192], replicated, may hold values from 0.5 to 1.5
- kv_weight: bfloat16 [8192, 2, 1024], P('dp', None, 'mp'), may hold values from -0.0625 to 0.0625
- action_query: bfloat16 [16, 128, 2048], P(('dp', 'segment'), None, 'mp'), may hold values from -104 to 104
- action_kv: bfloat16 [16, 128, 2, 1024], P(('dp', 'segment'), None, None, 'mp'), may hold values from -4.25 to 4.25
- out_cotangent: bfloat16 [16, 128, 2048], P(('dp', 'segment'), None, 'mp'), may hold values from -18 to 18
- prefix_blocks: int32 [16, 512], P(('dp', 'segment')), may hold values from 0 to 7, as said below
- action_blocks: int32 [16, 128], P(('dp', 'segment')), may hold values from 0 to 8, as said below
- prefix_lengths: int32 [16], P(('dp', 'segment')), may hold values from 128 to 512, as said below
- timesteps: int32 [16], P(('dp', 'segment')), may hold values from 0 to 999
Outputs:
- attn_out: bfloat16 [16, 128, 2048], P(('dp', 'segment'), None, 'mp')
- query_grad: float32 [16, 128, 2048], P(('dp', 'segment'), None, 'mp')
- action_kv_grad: float32 [16, 128, 2, 1024], P(('dp', 'segment'), None, None, 'mp')
- weight_grad: float32 [8192, 2, 1024], P('dp', None, 'mp')
Inputs may be any that keep to these rules, and one draw needn't show every extreme that they name: `prefix_blocks`: constant over each run of 64 positions, 0 on the first run, rising by 0 or 1 from one run to the next; in every draw some sample rises at every run. `action_blocks`: constant over each run of 64 positions; the last run of every sample holds 8; in every draw some sample's first run holds 0. `prefix_lengths`: in every draw some sample's prefix is whole and some sample's is 128.
All inputs are finite; a program needn't handle non-finite values.
Results may differ from a plain program's by a relative error of at most 0.017.
Values may be sent and summed in bfloat16 or wider, within the bound.
A program may use at most 128 MiB of HBM per device.

v0:
```python
import jax
import jax.numpy as jnp
from jax import lax
from jax.sharding import PartitionSpec as P

KVH = 8
HD = 128
QH = 16
STEPS = 1000
EPS = 1e-06
NEGATIVE = -1e30


def head_scores(query, keys):
    return jnp.einsum("agrh,jgh->graj", query, keys, preferred_element_type=jnp.float32) * HD ** (
        -0.5
    )


def backward_terms(probs, values, keys, query, grad_out):
    probs_low = probs.astype(jnp.bfloat16)
    d_probs = jnp.einsum("agrh,jgh->graj", grad_out, values, preferred_element_type=jnp.float32)
    delta = jnp.sum(probs * d_probs, axis=-1, keepdims=True)
    d_scores = (probs * (d_probs - delta)).astype(jnp.bfloat16)
    d_query = jnp.einsum(
        "graj,jgh->agrh", d_scores, keys, preferred_element_type=jnp.float32
    ) * HD ** (-0.5)
    d_keys = jnp.einsum(
        "graj,agrh->jgh", d_scores, query, preferred_element_type=jnp.float32
    ) * HD ** (-0.5)
    d_values = jnp.einsum("graj,agrh->jgh", probs_low, grad_out, preferred_element_type=jnp.float32)
    return (d_query, jnp.stack([d_keys, d_values], axis=1))


def shards(
    prefix_hidden,
    norm_gain,
    kv_weight,
    action_query,
    action_kv,
    out_cotangent,
    prefix_blocks,
    action_blocks,
    prefix_lengths,
    timesteps,
):
    acts = action_query.shape[1]
    heads_kv = kv_weight.shape[2] // HD
    ratio = QH // KVH
    columns = 2 * kv_weight.shape[2]
    wide = prefix_hidden[0].astype(jnp.float32)
    inverse = lax.rsqrt(jnp.mean(wide * wide, axis=-1, keepdims=True) + EPS)
    normed_local = (wide * inverse * norm_gain).astype(jnp.bfloat16)
    normed = lax.all_gather(normed_local, "mp", axis=0, tiled=True)
    rows = normed.shape[0]
    piece = lax.all_gather(kv_weight, "dp", axis=0, tiled=True)
    section = normed
    projected = jnp.dot(
        section, piece.reshape(piece.shape[0], columns), preferred_element_type=jnp.float32
    )
    prefix_kv = projected.astype(jnp.bfloat16).reshape(rows, 2, heads_kv, HD)
    own_pair = action_kv[0].reshape(acts, 2, heads_kv, HD)
    query = action_query[0].reshape(acts, heads_kv, ratio, HD)
    flow_weight = 0.5 + (timesteps[0].astype(jnp.float32) + 0.5) / STEPS
    grad_out = (
        (flow_weight * out_cotangent[0].astype(jnp.float32))
        .astype(jnp.bfloat16)
        .reshape(acts, heads_kv, ratio, HD)
    )
    pblocks = prefix_blocks[0]
    ablocks = action_blocks[0]
    length = prefix_lengths[0]
    keys = jnp.concatenate([prefix_kv[:, 0], own_pair[:, 0]], axis=0)
    values = jnp.concatenate([prefix_kv[:, 1], own_pair[:, 1]], axis=0)
    positions = jnp.arange(rows, dtype=jnp.int32)
    see_prefix = (pblocks[None, :] <= ablocks[:, None]) & (positions[None, :] < length)
    see_action = ablocks[None, :] <= ablocks[:, None]
    visible = jnp.concatenate([see_prefix, see_action], axis=1)
    masked = jnp.where(visible, head_scores(query, keys), NEGATIVE)
    top = jnp.max(masked, axis=-1, keepdims=True)
    expo = jnp.where(visible, jnp.exp(masked - top), 0.0)
    probs = expo / jnp.sum(expo, axis=-1, keepdims=True)
    out = jnp.einsum(
        "graj,jgh->agrh", probs.astype(jnp.bfloat16), values, preferred_element_type=jnp.float32
    )
    d_query, d_pair = backward_terms(probs, values, keys, query, grad_out)
    d_prefix = d_pair[:rows]
    d_action = d_pair[rows:]
    attn_out = out.astype(jnp.bfloat16).reshape(1, acts, ratio * heads_kv * HD)
    query_grad = d_query.reshape(1, acts, ratio * heads_kv * HD)
    action_kv_grad = d_action.reshape(1, acts, 2, heads_kv * HD)
    prefix_grad = d_prefix.astype(jnp.bfloat16).reshape(rows, columns)
    section = normed
    term = lax.dot_general(
        section, prefix_grad, (((0,), (0,)), ((), ())), preferred_element_type=jnp.float32
    )
    shard = lax.psum_scatter(
        term.reshape(kv_weight.shape[0] * lax.axis_size("dp"), 2, columns // 2).astype(
            jnp.bfloat16
        ),
        "dp",
        scatter_dimension=0,
        tiled=True,
    )
    weight_grad = lax.psum(shard, "segment").astype(jnp.float32)
    return (attn_out, query_grad, action_kv_grad, weight_grad)


def solution(mesh):
    placed = (
        P(("dp", "segment"), "mp", None),
        P(),
        P("dp", None, "mp"),
        P(("dp", "segment"), None, "mp"),
        P(("dp", "segment"), None, None, "mp"),
        P(("dp", "segment"), None, "mp"),
        P(("dp", "segment"), None),
        P(("dp", "segment"), None),
        P(("dp", "segment")),
        P(("dp", "segment")),
    )
    return jax.shard_map(
        shards,
        mesh=mesh,
        in_specs=placed,
        out_specs=(
            P(("dp", "segment"), None, "mp"),
            P(("dp", "segment"), None, "mp"),
            P(("dp", "segment"), None, None, "mp"),
            P("dp", None, "mp"),
        ),
        check_vma=False,
    )
```

profile of v0, /device:TPU:0, one launch (start us, length us, event | category | flops | bytes accessed | tf_op | source)
XLA Modules:
  0.0 657.0 jit_solution(16205726771575805277)
XLA Ops:
  7.2 0.0 all-gather.5.cloned.1.call-start
  7.2 0.7 all-gather.5.cloned.1.call-update
  7.9 0.0 all-gather.3.cloned.1.call-start
  8.0 6.4 copy.51
  14.3 3.5 fusion.1
  17.8 2.6 fusion.3
  20.5 0.0 copy-start.11
  20.5 0.0 all-gather.3.cloned.1.call-update
  20.5 0.0 reduce-scatter.2.cloned.1.call-start
  22.0 0.8 copy.88
  22.9 0.2 copy.87
  23.1 0.2 copy.53
  23.3 0.7 fusion.29
  24.0 0.1 copy.86
  24.1 0.1 broadcast_compare_fusion
  24.2 0.2 compare_and_fusion
  24.4 0.6 pad_add_fusion
  25.1 215.0 %all-gather.5.cloned.1.call-done = bf16[8192,2,512]{2,1,0:T(2,128)(2,1)} async-done(((bf16[1024,2,512]{2,1,0:T(2,128)(2,1)}), bf16[8192,2,512]{2,1,0:T(2,128)(2,1)}) %all-gather.5.cloned.1.call-update) | async-done | bytes 16777232 | tf_op jit(solution)/shard_map/all_gather | solution.py:56
  240.1 17.3 %copy.89 = bf16[1024,8,2,512]{3,1,2,0:T(8,128)(2,1)} copy(bf16[1024,8,2,512]{3,2,1,0:T(2,128)(2,1)} %bitcast.107) | data formatting | bytes 33554432
  257.5 1.1 all-gather.3.cloned.1.call-done
  258.5 14.8 %convolution_convert_fusion.1 = bf16[512,1024]{1,0:T(8,128)(2,1)S(1)} fusion(bf16[512,8192]{0,1:T(8,128)(2,1)} %all-gather.3.cloned.1.call-done, bf16[8192,1024]{1,0:T(8,128)(2,1)} %bitcast.108), kind=kOutput, calls=%fused_computation.20 | convolution fusion | flops 8590458880 | bytes 26214400 | tf_op jit(solution)/shard_map/dot_general | solution.py:58
  273.4 0.8 reshape.62
  274.2 0.4 fusion.28
  274.5 0.1 copy.91
  274.6 1.1 copy.84
  275.7 2.1 fusion.30
  277.9 0.0 copy-start.3
  277.9 0.0 copy-start.7
  277.9 1.8 convolution_bitcast_fusion
  279.7 0.1 copy-done.7
  279.8 0.1 copy-done.8
  279.9 0.6 fusion.5
  280.5 2.2 fusion.7
  282.7 0.5 fusion.11
  283.3 0.2 fusion.8
  283.4 16.1 %convolution_convert_fusion = bf16[8192,2,512]{2,0,1:T(8,128)(2,1)} fusion(bf16[2,512,512]{2,1,0:T(8,128)(2,1)S(1)} %bitcast.113, bf16[512,8192]{0,1:T(8,128)(2,1)} %all-gather.3.cloned.1.call-done), kind=kOutput, calls=%fused_computation.1 | convolution fusion | flops 8598323200 | bytes 26214400 | tf_op jit(solution)/shard_map/dot_general | solution.py:94
  299.5 0.0 reduce-scatter.2.cloned.1.call-update
  299.5 0.0 all-reduce.2.cloned.1.call-start
  299.6 280.8 %reduce-scatter.2.cloned.1.call-done = bf16[1024,2,512]{2,0,1:T(8,128)(2,1)} async-done(((bf16[8192,2,512]{2,0,1:T(8,128)(2,1)}), bf16[1024,2,512]{2,0,1:T(8,128)(2,1)}) %reduce-scatter.2.cloned.1.call-update) | async-done | bytes 2097168 | tf_op jit(solution)/shard_map/reduce_scatter | solution.py:97
  580.4 0.0 all-reduce.2.cloned.1.call-update
  580.5 2.3 convolution_convert_fusion.2
  582.8 0.9 copy.66
  583.6 1.2 convolution_multiply_fusion
  584.9 2.0 copy.67
  586.9 1.0 fusion.17
  588.0 1.0 copy.68
  589.0 55.8 %all-reduce.2.cloned.1.call-done = bf16[1024,2,512]{2,0,1:T(8,128)(2,1)} async-done(((bf16[1024,2,512]{2,0,1:T(8,128)(2,1)}), bf16[1024,2,512]{2,0,1:T(8,128)(2,1)}) %all-reduce.2.cloned.1.call-update) | async-done | bytes 2097168 | tf_op jit(solution)/shard_map/psum | solution.py:105
  644.7 5.8 copy.69
  (22 shorter events, 0.1 us)
Async XLA Ops:
  7.2 233.0 %all-gather.5.cloned.1.call-start = ((), (), s32[]{:S(2)}) async-start(), calls=%async_computation.2 | async-start | bytes 18874368 | tf_op jit(solution)/shard_map/all_gather | solution.py:56
  7.9 250.6 %all-gather.3.cloned.1.call-start = ((), (), s32[]{:S(2)}) async-start(), calls=%async_computation.1 | async-start | bytes 12582912 | tf_op jit(solution)/shard_map/all_gather | solution.py:54
  7.9 9.8 %copy-start.9 = (f32[8192]{0:T(1024)S(1)}, f32[8192]{0:T(1024)}, u32[]{:S(2)}) copy-start(f32[8192]{0:T(1024)} %param.11) | copy-start | bytes 98308
  14.3 3.5 copy-start
  20.4 1.5 copy-start.4
  20.4 2.4 copy-start.5
  20.4 2.6 copy-start.6
  20.4 3.7 copy-start.10
  20.5 3.8 copy-start.11
  20.5 559.9 %reduce-scatter.2.cloned.1.call-start = ((), (), s32[]{:S(2)}) async-start(), calls=%async_computation.3 | async-start | bytes 18874368 | tf_op jit(solution)/shard_map/reduce_scatter | solution.py:97
  277.9 1.9 copy-start.2
  277.9 1.9 copy-start.3
  277.9 1.9 copy-start.7
  277.9 2.0 copy-start.8
  279.7 3.5 copy-start.1
  299.5 345.2 %all-reduce.2.cloned.1.call-start = ((), (), s32[]{:S(2)}) async-start(), calls=%async_computation.4 | async-start | bytes 4194304 | tf_op jit(solution)/shard_map/psum | solution.py:105
Sparse Core Ops, SparseCore 0:
  10.1 229.9 all-gather.4
  242.2 16.2 all-gather.2
  299.7 280.7 reduce-scatter.1
  582.6 62.1 all-reduce.1
where the time goes:
time: 658 us; the launch traced here: 657 us
  waiting for transfers between devices  553 us (84%)
  matrix products  39.5 us (6%)
  local copies, waits for them, and re-layouts  38 us (6%)
  between operations  15.4 us (2%)
  other arithmetic  10.5 us (2%)
    reduce_scatter x1, waiting for transfers between devices, shards(): lax.psum_scatter(term.reshape(kv_weight.shape[0] * lax.axis_size('dp'), 2...  281 us
    all_gather x1, waiting for transfers between devices, shards(): piece = lax.all_gather(kv_weight, 'dp', axis=0, tiled=True)  215 us
    psum x1, waiting for transfers between devices, shards(): weight_grad = lax.psum(shard, 'segment').astype(jnp.float32)  55.8 us
    unnamed x34, local copies, waits for them, and re-layouts  35.1 us
    dot_general x1, matrix products, shards(): lax.dot_general(section, prefix_grad, (((0,), (0,)), ((), ())), preferred...  16.1 us
    dot_general x1, matrix products, shards(): jnp.dot(section, piece.reshape(piece.shape[0], columns), preferred_elemen...  14.8 us
  transfers between devices with their start and end apart: 4, of which 4 were waited for; matrix products, arithmetic and copies ran while one was open for 6% of the time, Pallas kernels for 0%

commit v1 on v0

--- a/solution.py
+++ b/solution.py
@@ -9,6 +9,11 @@
 STEPS = 1000
 EPS = 1e-06
 NEGATIVE = -1e30
+
+
+def add_the_other(block, axis):
+    received = lax.ppermute(block, axis, [(0, 1), (1, 0)])
+    return block + received
 
 
 def head_scores(query, keys):
@@ -102,7 +107,7 @@
         scatter_dimension=0,
         tiled=True,
     )
-    weight_grad = lax.psum(shard, "segment").astype(jnp.float32)
+    weight_grad = add_the_other(shard, "segment").astype(jnp.float32)
     return (attn_out, query_grad, action_kv_grad, weight_grad)
 
 

time: 658 us -> 642 us (0.976)
  waiting for transfers between devices: 553 us -> 535 us
    psum x1 -> x0, waiting for transfers between devices: 55.8 us -> none  [shards(): weight_grad = lax.psum(shard, 'segment').astype(jnp.float32)]
    ppermute x0 -> x1, waiting for transfers between devices: none -> 37.2 us  [add_the_other(): received = lax.ppermute(block, axis, [(0, 1), (1, 0)])]
where the time goes in v1:
time: 642 us
  waiting for transfers between devices  535 us (83%)
  matrix products  39.6 us (6%)
  local copies, waits for them, and re-layouts  37.4 us (6%)
  between operations  15.4 us (2%)
  other arithmetic  12.9 us (2%)
    reduce_scatter x1, waiting for transfers between devices, shards(): lax.psum_scatter(term.reshape(kv_weight.shape[0] * lax.axis_size('dp'), 2...  281 us
    all_gather x1, waiting for transfers between devices, shards(): piece = lax.all_gather(kv_weight, 'dp', axis=0, tiled=True)  215 us
    ppermute x1, waiting for transfers between devices, add_the_other(): received = lax.ppermute(block, axis, [(0, 1), (1, 0)])  37.2 us
    unnamed x34, local copies, waits for them, and re-layouts  34.6 us
    dot_general x1, matrix products, shards(): lax.dot_general(section, prefix_grad, (((0,), (0,)), ((), ())), preferred...  16.1 us
    dot_general x1, matrix products, shards(): jnp.dot(section, piece.reshape(piece.shape[0], columns), preferred_elemen...  14.9 us
  transfers between devices with their start and end apart: 4, of which 4 were waited for; matrix products, arithmetic and copies ran while one was open for 6% of the time, Pallas kernels for 0%

profile of v1, /device:TPU:0, one launch (start us, length us, event | category | flops | bytes accessed | tf_op | source)
XLA Modules:
  0.0 641.8 jit_solution(12233328159375121795)
XLA Ops:
  7.2 0.0 all-gather.5.cloned.1.call-start
  7.2 0.7 all-gather.5.cloned.1.call-update
  7.9 0.0 all-gather.3.cloned.1.call-start
  8.0 6.4 copy.51
  14.3 3.5 fusion.1
  17.8 2.6 fusion.3
  20.5 0.0 copy-start.11
  20.5 0.0 all-gather.3.cloned.1.call-update
  20.5 0.0 reduce-scatter.2.cloned.1.call-start
  22.0 0.8 copy.88
  22.9 0.2 copy.87
  23.1 0.2 copy.53
  23.3 0.7 fusion.29
  24.0 0.1 copy.86
  24.1 0.1 broadcast_compare_fusion
  24.2 0.2 compare_and_fusion
  24.4 0.6 pad_add_fusion
  25.1 215.0 %all-gather.5.cloned.1.call-done = bf16[8192,2,512]{2,1,0:T(2,128)(2,1)} async-done(((bf16[1024,2,512]{2,1,0:T(2,128)(2,1)}), bf16[8192,2,512]{2,1,0:T(2,128)(2,1)}) %all-gather.5.cloned.1.call-update) | async-done | bytes 16777232 | tf_op jit(solution)/shard_map/all_gather | solution.py:61
  240.1 17.3 %copy.89 = bf16[1024,8,2,512]{3,1,2,0:T(8,128)(2,1)} copy(bf16[1024,8,2,512]{3,2,1,0:T(2,128)(2,1)} %bitcast.107) | data formatting | bytes 33554432
  257.5 1.1 all-gather.3.cloned.1.call-done
  258.5 14.9 %convolution_convert_fusion.1 = bf16[512,1024]{1,0:T(8,128)(2,1)S(1)} fusion(bf16[512,8192]{0,1:T(8,128)(2,1)} %all-gather.3.cloned.1.call-done, bf16[8192,1024]{1,0:T(8,128)(2,1)} %bitcast.108), kind=kOutput, calls=%fused_computation.21 | convolution fusion | flops 8590458880 | bytes 26214400 | tf_op jit(solution)/shard_map/dot_general | solution.py:63
  273.4 0.8 reshape.62
  274.2 0.4 fusion.28
  274.5 0.1 copy.91
  274.6 1.1 copy.84
  275.7 2.1 fusion.30
  277.9 0.0 copy-start.3
  277.9 0.0 copy-start.7
  277.9 1.8 convolution_bitcast_fusion
  279.8 0.1 copy-done.7
  279.8 0.1 copy-done.8
  280.0 0.6 fusion.5
  280.6 2.2 fusion.7
  282.7 0.5 fusion.11
  283.3 0.2 fusion.8
  283.4 16.1 %convolution_convert_fusion = bf16[8192,2,512]{2,0,1:T(8,128)(2,1)} fusion(bf16[2,512,512]{2,1,0:T(8,128)(2,1)S(1)} %bitcast.113, bf16[512,8192]{0,1:T(8,128)(2,1)} %all-gather.3.cloned.1.call-done), kind=kOutput, calls=%fused_computation.1 | convolution fusion | flops 8598323200 | bytes 26214400 | tf_op jit(solution)/shard_map/dot_general | solution.py:99
  299.6 0.0 reduce-scatter.2.cloned.1.call-update
  299.6 280.8 %reduce-scatter.2.cloned.1.call-done = bf16[1024,2,512]{2,0,1:T(8,128)(2,1)} async-done(((bf16[8192,2,512]{2,0,1:T(8,128)(2,1)}), bf16[1024,2,512]{2,0,1:T(8,128)(2,1)}) %reduce-scatter.2.cloned.1.call-update) | async-done | bytes 2097168 | tf_op jit(solution)/shard_map/reduce_scatter | solution.py:102
  580.4 1.5 collective-permute-start
  581.9 2.3 convolution_convert_fusion.2
  584.2 0.9 copy.66
  585.1 1.2 convolution_multiply_fusion
  586.3 2.0 copy.67
  588.3 1.0 fusion.17
  589.3 1.0 copy.68
  590.3 37.2 %collective-permute-done = bf16[1024,2,512]{2,0,1:T(8,128)(2,1)} collective-permute-done((bf16[1024,2,512]{2,0,1:T(8,128)(2,1)}, bf16[1024,2,512]{2,0,1:T(8,128)(2,1)}, u32[]{:S(2)}, u32[]{:S(2)}) %collective-permute-start) | collective-permute-done | bytes 2097184 | tf_op jit(solution)/shard_map/ppermute | solution.py:15
  627.5 2.5 add_convert_fusion
  630.0 5.2 copy.69
  (22 shorter events, 0.1 us)
Async XLA Ops:
  7.2 233.0 %all-gather.5.cloned.1.call-start = ((), (), s32[]{:S(2)}) async-start(), calls=%async_computation.2 | async-start | bytes 18874368 | tf_op jit(solution)/shard_map/all_gather | solution.py:61
  7.9 250.6 %all-gather.3.cloned.1.call-start = ((), (), s32[]{:S(2)}) async-start(), calls=%async_computation.1 | async-start | bytes 12582912 | tf_op jit(solution)/shard_map/all_gather | solution.py:59
  7.9 9.8 %copy-start.9 = (f32[8192]{0:T(1024)S(1)}, f32[8192]{0:T(1024)}, u32[]{:S(2)}) copy-start(f32[8192]{0:T(1024)} %param.11) | copy-start | bytes 98308
  14.3 3.5 copy-start
  20.4 1.5 copy-start.4
  20.4 2.4 copy-start.5
  20.4 2.6 copy-start.6
  20.4 3.7 copy-start.10
  20.5 3.8 copy-start.11
  20.5 559.9 %reduce-scatter.2.cloned.1.call-start = ((), (), s32[]{:S(2)}) async-start(), calls=%async_computation.3 | async-start | bytes 18874368 | tf_op jit(solution)/shard_map/reduce_scatter | solution.py:102
  277.9 1.9 copy-start.2
  277.9 1.9 copy-start.3
  277.9 1.9 copy-start.7
  277.9 2.0 copy-start.8
  279.7 3.5 copy-start.1
  580.4 47.1 %collective-permute-start = (bf16[1024,2,512]{2,0,1:T(8,128)(2,1)}, bf16[1024,2,512]{2,0,1:T(8,128)(2,1)}, u32[]{:S(2)}, u32[]{:S(2)}) collective-permute-start(bf16[1024,2,512]{2,0,1:T(8,128)(2,1)} %reduce-scatter.2.cloned.1.call-done), channel_id=1, source_target_pairs={{0,2},{2,0},{1,3},{3,1},{4,6},{6,4},{5,7},{7,5},{8,10},{10,8},{9,1... | collective-permute-start | bytes 6291464 | tf_op jit(solution)/shard_map/ppermute | solution.py:15
Sparse Core Ops, SparseCore 0:
  10.1 229.9 all-gather.4
  242.2 16.2 all-gather.2
  299.7 280.6 reduce-scatter.1
